TPU v7x, 512 devices: a whole 4x4x16 slice. The times are simulated.
512 devices in a mesh: dp: 4 (over z_lo), row: 8 (over y, core), col: 16 (over z_hi, x).
Axes of the slice: x: 4, y: 4, z: 16 (z_hi: 4, z_lo: 4; z = z_hi * 4 + z_lo), core: 2. Of those that a mesh axis runs over, the one named last changes fastest.
Arguments:
- queries: bfloat16 [4, 64, 256, 768], P('dp', 'row', 'col'), may hold values from -5.5 to 5.5
- keys: bfloat16 [4, 64, 256, 768], P('dp', 'row', 'col'), may hold values from -5.5 to 5.5
- values: bfloat16 [4, 64, 256, 768], P('dp', 'row', 'col'), may hold values from -6 to 6
- occupancy: int32 [4, 8, 32], P('dp', 'row', 'col'), may hold values from 0 to 64, as said below
- out_weight: bfloat16 [768, 768], P('dp'), may hold values from -0.21875 to 0.21875
- grad_out: bfloat16 [4, 64, 256, 768], P('dp', 'row', 'col'), may hold values from -6 to 6
Outputs:
- grad_queries: bfloat16 [4, 64, 256, 768], P('dp', 'row', 'col')
- grad_keys: bfloat16 [4, 64, 256, 768], P('dp', 'row', 'col')
- grad_values: bfloat16 [4, 64, 256, 768], P('dp', 'row', 'col')
- grad_weight: float32 [768, 768], P('dp')
Inputs may be any that keep to these rules, and one draw needn't show every extreme that they name: `occupancy`: the occupied tiles of a block are its first that many tiles, row by row over its 8 x 8 tiles. Every slide has a block holding 8 * 8 and a block holding 0.
All inputs are finite; a program needn't handle non-finite values.
Results may differ from a plain program's by a relative error of at most 0.02.
Values may be sent and summed in bfloat16 or wider, within the bound.
A program may use at most 64 MiB of HBM per device.

v0:
```python
import jax
import jax.numpy as jnp
from jax import lax
from jax.sharding import PartitionSpec as P

HEAD_DIM = 64
SIDE = 8
REACH = 3
NEG = -1e30


def passed_along(value, axis, steps):
    count = lax.axis_size(axis)
    leading, last = (max(0, -steps), min(count, count - steps))
    return lax.ppermute(value, axis, [(source, source + steps) for source in range(leading, last)])


def for_sending(value):
    return jax.tree.map(lambda a: a.astype(jnp.bfloat16) if a.dtype == jnp.float32 else a, value)


def extended(cells, sides, width):
    for axis, dim in sides:
        count = lax.axis_size(axis)
        ends = count - 1
        head = lax.slice_in_dim(cells, 0, width, axis=dim)
        tail = lax.slice_in_dim(cells, cells.shape[dim] - width, cells.shape[dim], axis=dim)
        cells = jnp.concatenate(
            [
                lax.ppermute(tail, axis, [(i, (i + 1) % count) for i in range(ends)]),
                cells,
                lax.ppermute(head, axis, [((i + 1) % count, i) for i in range(ends)]),
            ],
            axis=dim,
        )
    return cells


def product(form, left, right):
    return jnp.einsum(form, left, right, preferred_element_type=jnp.float32)


def near_table(block_side, radius):
    window = block_side + 2 * radius
    queries_at = jnp.arange(block_side * block_side)
    keys_at = jnp.arange(window * window)
    row_gap = keys_at[None, :] // window - queries_at[:, None] // block_side - radius
    col_gap = keys_at[None, :] % window - queries_at[:, None] % block_side - radius
    return (jnp.abs(row_gap) <= radius) & (jnp.abs(col_gap) <= radius)


def tile_valid(counts, block_side):
    inside = jnp.arange(block_side * block_side, dtype=jnp.int32).reshape(block_side, block_side)
    flags = inside[None, :, None, :] < counts[:, None, :, None]
    return flags.reshape(counts.shape[0] * block_side, counts.shape[1] * block_side).astype(
        jnp.float32
    )


def blockify(source, block_side):
    height, breadth = (source.shape[0], source.shape[1])
    others = source.shape[2:]
    shaped = source.reshape(
        (height // block_side, block_side, breadth // block_side, block_side) + others
    )
    shaped = jnp.swapaxes(shaped, 1, 2)
    return shaped.reshape(
        (height // block_side, breadth // block_side, block_side * block_side) + others
    )


def unblock(source, block_side):
    block_rows, block_cols = (source.shape[0], source.shape[1])
    others = source.shape[3:]
    shaped = source.reshape((block_rows, block_cols, block_side, block_side) + others)
    shaped = jnp.swapaxes(shaped, 1, 2)
    return shaped.reshape((block_rows * block_side, block_cols * block_side) + others)


def cut_axis(source, dimension, block_side, radius, number):
    padding = [(0, 0)] * source.ndim
    padding[dimension] = (0, block_side - 2 * radius)
    shaped = jnp.pad(source, padding)
    shaped = shaped.reshape(
        source.shape[:dimension] + (number + 1, block_side) + source.shape[dimension + 1 :]
    )
    leading = lax.slice_in_dim(shaped, 0, number, axis=dimension)
    trailing = lax.slice_in_dim(
        lax.slice_in_dim(shaped, 1, number + 1, axis=dimension), 0, 2 * radius, axis=dimension + 1
    )
    return jnp.concatenate([leading, trailing], axis=dimension + 1)


def windows(source, block_side, radius, block_rows, block_cols):
    window = block_side + 2 * radius
    shaped = cut_axis(source, 0, block_side, radius, block_rows)
    shaped = cut_axis(shaped, 2, block_side, radius, block_cols)
    shaped = jnp.swapaxes(shaped, 1, 2)
    return shaped.reshape((block_rows * block_cols, window * window) + source.shape[2:])


def merge_axis(source, dimension, block_side, radius, number):
    leading = lax.slice_in_dim(source, 0, block_side, axis=dimension + 1)
    trailing = lax.slice_in_dim(source, block_side, block_side + 2 * radius, axis=dimension + 1)
    lead_pad = [(0, 0)] * source.ndim
    lead_pad[dimension] = (0, 1)
    trail_pad = [(0, 0)] * source.ndim
    trail_pad[dimension] = (1, 0)
    trail_pad[dimension + 1] = (0, block_side - 2 * radius)
    summed = jnp.pad(leading, lead_pad) + jnp.pad(trailing, trail_pad)
    summed = summed.reshape(
        source.shape[:dimension] + ((number + 1) * block_side,) + source.shape[dimension + 2 :]
    )
    return lax.slice_in_dim(summed, 0, number * block_side + 2 * radius, axis=dimension)


def fold_back(source, block_side, radius, block_rows, block_cols):
    window = block_side + 2 * radius
    shaped = source.reshape((block_rows, block_cols, window, window) + source.shape[2:])
    shaped = jnp.swapaxes(shaped, 1, 2)
    shaped = merge_axis(shaped, 2, block_side, radius, block_cols)
    return merge_axis(shaped, 0, block_side, radius, block_rows)


def attend(query_blocks, key_win, value_win, key_flag, query_flag, nearby, scaling):
    scores = product("nqhd,nkhd->nhqk", query_blocks, key_win) * scaling
    allowed = nearby[None, None] & (key_flag[:, None, None, :] > 0)
    masked = jnp.where(allowed, scores, NEG)
    highest = jnp.max(masked, axis=-1, keepdims=True)
    raised = jnp.exp(masked - highest)
    inverse = 1.0 / jnp.sum(raised, axis=-1, keepdims=True)
    weights = raised * inverse
    rounded = weights.astype(jnp.bfloat16)
    mixed = product("nhqk,nkhd->nqhd", rounded, value_win)
    attended = (mixed * query_flag[:, :, None, None]).astype(jnp.bfloat16)
    return (attended, weights, rounded, highest, inverse)


def query_side(weights, grad_blocks, key_win, value_win, scaling):
    prob_grad = product("nqhd,nkhd->nhqk", grad_blocks, value_win)
    correction = jnp.sum(weights * prob_grad, axis=-1, keepdims=True)
    score_grad = (weights * (prob_grad - correction) * scaling).astype(jnp.bfloat16)
    query_grad = product("nhqk,nkhd->nqhd", score_grad, key_win)
    return (query_grad, score_grad, correction)


def return_rims(key_full, value_full):
    middle = (key_full[REACH:-REACH], value_full[REACH:-REACH])
    for offset in (1, -1):
        if offset == 1:
            border = (key_full[-REACH:], value_full[-REACH:])
        else:
            border = (key_full[:REACH], value_full[:REACH])
        arrived = (
            passed_along(border[0].astype(jnp.bfloat16), "row", offset).astype(jnp.float32),
            passed_along(border[1].astype(jnp.bfloat16), "row", offset).astype(jnp.float32),
        )
        if offset == 1:
            middle = tuple(
                (portion.at[:REACH].add(incoming) for portion, incoming in zip(middle, arrived))
            )
        else:
            middle = tuple(
                (portion.at[-REACH:].add(incoming) for portion, incoming in zip(middle, arrived))
            )
    centre = tuple((portion[:, REACH:-REACH] for portion in middle))
    for offset in (1, -1):
        if offset == 1:
            border = tuple((portion[:, -REACH:] for portion in middle))
        else:
            border = tuple((portion[:, :REACH] for portion in middle))
        arrived = jax.tree.map(
            lambda part, own: part.astype(own.dtype),
            passed_along(for_sending(border), "col", offset),
            border,
        )
        if offset == 1:
            centre = tuple(
                (portion.at[:, :REACH].add(incoming) for portion, incoming in zip(centre, arrived))
            )
        else:
            centre = tuple(
                (portion.at[:, -REACH:].add(incoming) for portion, incoming in zip(centre, arrived))
            )
    return centre


def on_device(queries, keys, values, occupancy, out_weight, grad_out):
    query_tiles = queries[0]
    key_tiles = keys[0]
    value_tiles = values[0]
    grad_tiles = grad_out[0]
    counts = occupancy[0]
    height, breadth, channels = query_tiles.shape
    out_width = grad_tiles.shape[2]
    head_count = channels // HEAD_DIM
    block_rows = height // SIDE
    block_cols = breadth // SIDE
    block_count = block_rows * block_cols
    block_area = SIDE * SIDE
    window = SIDE + 2 * REACH
    window_area = window * window
    tile_count = height * breadth
    nearby = near_table(SIDE, REACH)
    scaling = HEAD_DIM ** (-0.5)
    occupied = tile_valid(counts, SIDE)
    key_ext, value_ext, flag_ext = (
        extended(key_tiles, (("row", 0), ("col", 1)), REACH),
        extended(value_tiles, (("row", 0), ("col", 1)), REACH),
        extended(occupied.astype(jnp.bfloat16), (("row", 0), ("col", 1)), REACH),
    )
    key_win = windows(key_ext, SIDE, REACH, block_rows, block_cols).reshape(
        block_count, window_area, head_count, HEAD_DIM
    )
    value_win = windows(value_ext, SIDE, REACH, block_rows, block_cols).reshape(
        block_count, window_area, head_count, HEAD_DIM
    )
    flag_win = windows(flag_ext, SIDE, REACH, block_rows, block_cols)
    query_blocks = blockify(query_tiles, SIDE).reshape(
        block_count, block_area, head_count, HEAD_DIM
    )
    query_flag = blockify(occupied, SIDE).reshape(block_count, block_area)
    attended, weights, rounded, highest, inverse = attend(
        query_blocks, key_win, value_win, flag_win, query_flag, nearby, scaling
    )
    flat_grads = grad_tiles.reshape(tile_count, out_width)
    out_back = lax.dot_general(
        flat_grads,
        lax.all_gather(out_weight, "dp", axis=0, tiled=True),
        (((1,), (1,)), ((), ())),
        preferred_element_type=jnp.float32,
    )
    gated_grad = out_back.astype(jnp.bfloat16).reshape(height, breadth, channels) * occupied[
        :, :, None
    ].astype(jnp.bfloat16)
    grad_blocks = blockify(gated_grad, SIDE).reshape(block_count, block_area, head_count, HEAD_DIM)
    out_blocks = blockify(grad_tiles, SIDE).reshape(tile_count, out_width)
    weight_term = lax.dot_general(
        attended.reshape(tile_count, channels),
        out_blocks,
        (((0,), (0,)), ((), ())),
        preferred_element_type=jnp.float32,
    )
    summed = lax.psum(weight_term, ("row", "col"))
    slide_part = lax.psum_scatter(
        summed.astype(jnp.bfloat16), "dp", scatter_dimension=0, tiled=True
    ).astype(jnp.float32)
    all_tiles = tile_count * lax.axis_size("dp") * lax.axis_size("row") * lax.axis_size("col")
    grad_weight = slide_part * all_tiles ** (-0.5)
    query_grad, score_grad, correction = query_side(
        weights, grad_blocks, key_win, value_win, scaling
    )
    key_part = product("nhqk,nqhd->nkhd", score_grad, query_blocks).reshape(
        block_count, window_area, channels
    )
    value_part = product("nhqk,nqhd->nkhd", rounded, grad_blocks).reshape(
        block_count, window_area, channels
    )
    key_full = fold_back(key_part, SIDE, REACH, block_rows, block_cols)
    value_full = fold_back(value_part, SIDE, REACH, block_rows, block_cols)
    key_sum, value_sum = return_rims(key_full, value_full)
    grad_query = unblock(query_grad.reshape(block_rows, block_cols, block_area, channels), SIDE)
    return (
        grad_query.astype(jnp.bfloat16)[None],
        key_sum.astype(jnp.bfloat16)[None],
        value_sum.astype(jnp.bfloat16)[None],
        grad_weight,
    )


def solution(mesh):
    return jax.shard_map(
        on_device,
        mesh=mesh,
        in_specs=(
            P("dp", "row", "col", None),
            P("dp", "row", "col", None),
            P("dp", "row", "col", None),
            P("dp", "row", "col"),
            P("dp", None),
            P("dp", "row", "col", None),
        ),
        out_specs=(
            P("dp", "row", "col", None),
            P("dp", "row", "col", None),
            P("dp", "row", "col", None),
            P("dp", None),
        ),
        check_vma=False,
    )
```

profile of v0, /device:TPU:39, one launch (start us, length us, event | category | flops | bytes accessed | tf_op | source)
XLA Modules:
  0.0 1018.1 jit_solution(9643661524782293680)
XLA Ops:
  8.3 2.6 collective-permute-start.1
  10.9 3.1 collective-permute-start
  19.8 3.6 collective-permute-start.4
  27.3 2.4 collective-permute-start.7
  29.7 8.8 collective-permute-start.6
  38.6 3.0 collective-permute-start.8
  44.1 9.4 collective-permute-start.2
  55.6 9.4 collective-permute-start.10
  66.7 9.1 collective-permute-done.11
  80.4 2.4 fusion.67
  88.0 4.9 fusion.24
  95.6 764.2 %all-reduce.15 = bf16[768,768]{1,0:T(8,128)(2,1)} all-reduce(f32[768,768]{1,0:T(8,128)S(1)} %fusion.69), channel_id=1, replica_groups=mesh['dp'=4,'row'=8,'col'=16] {'row','col'}, use_global_device_ids=true, to_apply=%region_3.4 | all-reduce | flops 589824 | bytes 3538944 | tf_op jit(solution)/shard_map/psum | solution.py:244
  864.2 11.5 %fusion.25 = bf16[2,64,12,64]{1,3,2,0:T(8,128)(2,1)} fusion(bf16[2,196,12,64]{1,3,2,0:T(8,128)(2,1)S(1)} %copy.80, f32[2,12,64,196]{3,2,1,0:T(8,128)} %fusion.68, f32[2,12,64,196]{3,2,1,0:T(8,128)} %get-tuple-element.127, f32[2,12,64]{2,1,0:T(8,128)S(1)} %broadcast_divide_fusion), kind=kOutput, calls=%fused_computation.21 | convolution fusion | flops 40742596 | bytes 3213312 | tf_op jit(solution)/shard_map/nhqk,nkhd->nqhd/dot_general | solution.py:40
  875.7 11.9 %fusion.12 = f32[2,196,12,64]{1,3,2,0:T(8,128)} fusion(bf16[2,64,12,64]{1,3,2,0:T(8,128)(2,1)S(1)} %copy-done.10, f32[2,12,64,196]{3,2,1,0:T(8,128)} %fusion.68, f32[2,12,64,196]{3,2,1,0:T(8,128)} %get-tuple-element.127, f32[2,12,64]{2,1,0:T(8,128)S(1)} %broadcast_divide_fusion), kind=kOutput, calls=%fused_computation.9 | convolution fusion | flops 40644292 | bytes 3815424 | tf_op jit(solution)/shard_map/nhqk,nqhd->nkhd/dot_general | solution.py:40
  887.7 3.5 copy.84
  897.9 5.8 convolution_bitcast_fusion
  903.7 3.5 copy.87
  917.1 51.0 %collective-permute-start.13 = (bf16[3,22,768]{2,1,0:T(8,128)(2,1)S(1)}, bf16[3,22,768]{2,1,0:T(8,128)(2,1)S(1)}, u32[]{:S(2)}, u32[]{:S(2)}) collective-permute-start(bf16[3,22,768]{2,1,0:T(8,128)(2,1)S(1)} %get-tuple-element.102), channel_id=1, source_target_pairs={{16,0},{32,16},{48,32},{64,48},{80,64},{96,80},{112,96},{17,1},{33... | collective-permute-start | bytes 304136 | tf_op jit(solution)/shard_map/ppermute | solution.py:15
  970.0 2.4 collective-permute-start.17
  972.7 3.4 collective-permute-done.17
  976.3 9.0 collective-permute-start.14
  985.3 3.1 collective-permute-start.15
  988.5 8.2 collective-permute-start.18
  999.8 7.9 collective-permute-done.19
  (182 shorter events, 58.9 us)
Async XLA Ops:
  7.2 852.7 %all-gather.2.cloned.1.call-start = ((), (), s32[]{:S(2)}) async-start(), calls=%async_computation.1 | async-start | bytes 1474560 | tf_op jit(solution)/shard_map/all_gather | solution.py:229
  8.3 33.8 %collective-permute-start.1 = (bf16[3,16,768]{2,1,0:T(8,128)(2,1)S(1)}, bf16[3,16,768]{2,1,0:T(8,128)(2,1)S(1)}, u32[]{:S(2)}, u32[]{:S(2)}) collective-permute-start(bf16[3,16,768]{2,1,0:T(8,128)(2,1)S(1)} %get-tuple-element.119), channel_id=1, source_target_pairs={{16,0},{32,16},{48,32},{64,48},{80,64},{96,80},{112,96},{17,1},{33... | collective-permute-start | bytes 221192 | tf_op jit(solution)/shard_map/ppermute | solution.py:32
  10.9 31.2 %collective-permute-start = (bf16[3,16,768]{2,1,0:T(8,128)(2,1)S(1)}, bf16[3,16,768]{2,1,0:T(8,128)(2,1)S(1)}, u32[]{:S(2)}, u32[]{:S(2)}) collective-permute-start(bf16[3,16,768]{2,1,0:T(8,128)(2,1)S(1)} %get-tuple-element.118), channel_id=1, source_target_pairs={{0,16},{16,32},{32,48},{48,64},{64,80},{80,96},{96,112},{1,17},{17... | collective-permute-start | bytes 221192 | tf_op jit(solution)/shard_map/ppermute | solution.py:30
  14.0 995.5 %reduce-scatter.2.cloned.1.call-start = ((), (), s32[]{:S(2)}) async-start(), calls=%async_computation.2 | async-start | bytes 1474560 | tf_op jit(solution)/shard_map/reduce_scatter | solution.py:245
  15.0 38.5 %collective-permute-start.9 = (bf16[3,16,768]{2,1,0:T(8,128)(2,1)S(1)}, bf16[3,16,768]{2,1,0:T(8,128)(2,1)S(1)}, u32[]{:S(2)}, u32[]{:S(2)}) collective-permute-start(bf16[3,16,768]{2,1,0:T(8,128)(2,1)S(1)} %get-tuple-element.117), channel_id=1, source_target_pairs={{16,0},{32,16},{48,32},{64,48},{80,64},{96,80},{112,96},{17,1},{33... | collective-permute-start | bytes 221192 | tf_op jit(solution)/shard_map/ppermute | solution.py:32
  17.9 9.3 collective-permute-start.5
  19.8 7.4 collective-permute-start.4
  26.3 56.6 %copy-start.9 = (bf16[2,64,12,64]{1,3,2,0:T(8,128)(2,1)}, bf16[2,64,12,64]{1,3,2,0:T(8,128)(2,1)S(1)}, u32[]{:S(2)}) copy-start(bf16[2,64,12,64]{1,3,2,0:T(8,128)(2,1)S(1)} %copy.83) | copy-start | bytes 589828
  27.3 11.3 %collective-permute-start.7 = (bf16[14,3]{1,0:T(8,128)(2,1)S(1)}, bf16[14,3]{1,0:T(8,128)(2,1)S(1)}, u32[]{:S(2)}, u32[]{:S(2)}) collective-permute-start(bf16[14,3]{1,0:T(8,128)(2,1)S(1)} %get-tuple-element.123), channel_id=1, source_target_pairs={{1,0},{2,1},{3,2},{4,3},{5,4},{6,5},{7,6},{8,7},{9,8},{10,9},{11,1... | collective-permute-start | bytes 260 | tf_op jit(solution)/shard_map/ppermute | solution.py:32
  29.7 11.8 %collective-permute-start.6 = (bf16[14,3]{1,0:T(8,128)(2,1)S(1)}, bf16[14,3]{1,0:T(8,128)(2,1)S(1)}, u32[]{:S(2)}, u32[]{:S(2)}) collective-permute-start(bf16[14,3]{1,0:T(8,128)(2,1)S(1)} %get-tuple-element.122), channel_id=1, source_target_pairs={{0,1},{1,2},{2,3},{3,4},{4,5},{5,6},{6,7},{7,8},{8,9},{9,10},{10,1... | collective-permute-start | bytes 260 | tf_op jit(solution)/shard_map/ppermute | solution.py:30
  38.6 14.9 %collective-permute-start.8 = (bf16[3,16,768]{2,1,0:T(8,128)(2,1)S(1)}, bf16[3,16,768]{2,1,0:T(8,128)(2,1)S(1)}, u32[]{:S(2)}, u32[]{:S(2)}) collective-permute-start(bf16[3,16,768]{2,1,0:T(8,128)(2,1)S(1)} %get-tuple-element.116), channel_id=1, source_target_pairs={{0,16},{16,32},{32,48},{48,64},{64,80},{80,96},{96,112},{1,17},{17... | collective-permute-start | bytes 221192 | tf_op jit(solution)/shard_map/ppermute | solution.py:30
  42.2 24.1 %collective-permute-start.3 = (bf16[14,3,768]{2,1,0:T(4,128)(2,1)S(1)}, bf16[14,3,768]{2,1,0:T(4,128)(2,1)S(1)}, u32[]{:S(2)}, u32[]{:S(2)}) collective-permute-start(bf16[14,3,768]{2,1,0:T(4,128)(2,1)S(1)} %get-tuple-element.111), channel_id=1, source_target_pairs={{1,0},{2,1},{3,2},{4,3},{5,4},{6,5},{7,6},{8,7},{9,8},{10,9},{11,1... | collective-permute-start | bytes 193544 | tf_op jit(solution)/shard_map/ppermute | solution.py:32
  44.1 22.2 %collective-permute-start.2 = (bf16[14,3,768]{2,1,0:T(4,128)(2,1)S(1)}, bf16[14,3,768]{2,1,0:T(4,128)(2,1)S(1)}, u32[]{:S(2)}, u32[]{:S(2)}) collective-permute-start(bf16[14,3,768]{2,1,0:T(4,128)(2,1)S(1)} %get-tuple-element.110), channel_id=1, source_target_pairs={{0,1},{1,2},{2,3},{3,4},{4,5},{5,6},{6,7},{7,8},{8,9},{9,10},{10,1... | collective-permute-start | bytes 193544 | tf_op jit(solution)/shard_map/ppermute | solution.py:30
  53.6 22.2 %collective-permute-start.11 = (bf16[14,3,768]{2,1,0:T(4,128)(2,1)S(1)}, bf16[14,3,768]{2,1,0:T(4,128)(2,1)S(1)}, u32[]{:S(2)}, u32[]{:S(2)}) collective-permute-start(bf16[14,3,768]{2,1,0:T(4,128)(2,1)S(1)} %get-tuple-element.109), channel_id=1, source_target_pairs={{1,0},{2,1},{3,2},{4,3},{5,4},{6,5},{7,6},{8,7},{9,8},{10,9},{11,1... | collective-permute-start | bytes 193544 | tf_op jit(solution)/shard_map/ppermute | solution.py:32
  55.6 20.3 %collective-permute-start.10 = (bf16[14,3,768]{2,1,0:T(4,128)(2,1)S(1)}, bf16[14,3,768]{2,1,0:T(4,128)(2,1)S(1)}, u32[]{:S(2)}, u32[]{:S(2)}) collective-permute-start(bf16[14,3,768]{2,1,0:T(4,128)(2,1)S(1)} %get-tuple-element.108), channel_id=1, source_target_pairs={{0,1},{1,2},{2,3},{3,4},{4,5},{5,6},{6,7},{7,8},{8,9},{9,10},{10,1... | collective-permute-start | bytes 193544 | tf_op jit(solution)/shard_map/ppermute | solution.py:30
  95.6 764.3 %copy-start.15 = (bf16[1,8,16,768]{3,2,1,0:T(8,128)(2,1)S(1)}, bf16[1,8,16,768]{3,2,1,0:T(8,128)(2,1)}, u32[]{:S(2)}) copy-start(bf16[1,8,16,768]{3,2,1,0:T(8,128)(2,1)} %param.27) | copy-start | bytes 589828
  914.9 57.5 %collective-permute-start.12 = (bf16[3,22,768]{2,1,0:T(8,128)(2,1)S(1)}, bf16[3,22,768]{2,1,0:T(8,128)(2,1)S(1)}, u32[]{:S(2)}, u32[]{:S(2)}) collective-permute-start(bf16[3,22,768]{2,1,0:T(8,128)(2,1)S(1)} %get-tuple-element.103), channel_id=1, source_target_pairs={{0,16},{16,32},{32,48},{48,64},{64,80},{80,96},{96,112},{1,17},{17... | collective-permute-start | bytes 304136 | tf_op jit(solution)/shard_map/ppermute | solution.py:15
  917.1 55.4 %collective-permute-start.13 = (bf16[3,22,768]{2,1,0:T(8,128)(2,1)S(1)}, bf16[3,22,768]{2,1,0:T(8,128)(2,1)S(1)}, u32[]{:S(2)}, u32[]{:S(2)}) collective-permute-start(bf16[3,22,768]{2,1,0:T(8,128)(2,1)S(1)} %get-tuple-element.102), channel_id=1, source_target_pairs={{16,0},{32,16},{48,32},{64,48},{80,64},{96,80},{112,96},{17,1},{33... | collective-permute-start | bytes 304136 | tf_op jit(solution)/shard_map/ppermute | solution.py:15
  968.1 4.4 collective-permute-start.16
  970.0 6.1 collective-permute-start.17
  976.3 22.3 %collective-permute-start.14 = (bf16[8,3,768]{2,1,0:T(4,128)(2,1)S(1)}, bf16[8,3,768]{2,1,0:T(4,128)(2,1)S(1)}, u32[]{:S(2)}, u32[]{:S(2)}) collective-permute-start(bf16[8,3,768]{2,1,0:T(4,128)(2,1)S(1)} %get-tuple-element.115), channel_id=1, source_target_pairs={{0,1},{1,2},{2,3},{3,4},{4,5},{5,6},{6,7},{7,8},{8,9},{9,10},{10,1... | collective-permute-start | bytes 110600 | tf_op jit(solution)/shard_map/ppermute | solution.py:15
  985.3 13.8 %collective-permute-start.15 = (bf16[8,3,768]{2,1,0:T(4,128)(2,1)S(1)}, bf16[8,3,768]{2,1,0:T(4,128)(2,1)S(1)}, u32[]{:S(2)}, u32[]{:S(2)}) collective-permute-start(bf16[8,3,768]{2,1,0:T(4,128)(2,1)S(1)} %get-tuple-element.114), channel_id=1, source_target_pairs={{1,0},{2,1},{3,2},{4,3},{5,4},{6,5},{7,6},{8,7},{9,8},{10,9},{11,1... | collective-permute-start | bytes 110600 | tf_op jit(solution)/shard_map/ppermute | solution.py:15
  988.5 10.2 collective-permute-start.18
  996.7 11.1 %collective-permute-start.19 = (bf16[8,3,768]{2,1,0:T(4,128)(2,1)S(1)}, bf16[8,3,768]{2,1,0:T(4,128)(2,1)S(1)}, u32[]{:S(2)}, u32[]{:S(2)}) collective-permute-start(bf16[8,3,768]{2,1,0:T(4,128)(2,1)S(1)} %get-tuple-element.112), channel_id=1, source_target_pairs={{1,0},{2,1},{3,2},{4,3},{5,4},{6,5},{7,6},{8,7},{9,8},{10,9},{11,1... | collective-permute-start | bytes 110600 | tf_op jit(solution)/shard_map/ppermute | solution.py:15
  (19 other events, 153.0 us)
Sparse Core Ops, SparseCore 0:
  14.1 41.7 all-gather.1
  860.0 89.8 reduce-scatter.1
where the time goes:
time: 1020 us
  blocking collectives  764 us (75%)
  starting transfers between devices  130 us (13%)
  matrix products  43 us (4%)
  local copies, waits for them, and re-layouts  35 us (3%)
  waiting for transfers between devices  21.9 us (2%)
  between operations  15.1 us (1%)
    psum x1, blocking collectives, on_device(): summed = lax.psum(weight_term, ('row', 'col'))  764 us
    ppermute x8, starting transfers between devices, passed_along(): lax.ppermute(value, axis, [(source, source + steps) for source in range(l...  79.4 us
    ppermute x6, starting transfers between devices, extended(): lax.ppermute(tail, axis, [(i, (i + 1) % count) for i in range(ends)])  37.3 us
    dot_general x6, matrix products, product(): return jnp.einsum(form, left, right, preferred_element_type=jnp.float32)  37.2 us
  transfers between devices with their start and end apart: 22, of which 4 were waited for; matrix products, arithmetic and copies ran while one was open for 8% of the time, Pallas kernels for 0%

commit v1 on v0

--- a/solution.py
+++ b/solution.py
@@ -241,7 +241,7 @@
         (((0,), (0,)), ((), ())),
         preferred_element_type=jnp.float32,
     )
-    summed = lax.psum(weight_term, ("row", "col"))
+    summed = lax.psum(lax.psum(weight_term, "row"), "col")
     slide_part = lax.psum_scatter(
         summed.astype(jnp.bfloat16), "dp", scatter_dimension=0, tiled=True
     ).astype(jnp.float32)

time: 1020 us -> 518 us (0.51)
  the two profiles are of different devices: /device:TPU:39 before, /device:TPU:47 now
where the time goes in v1:
time: 518 us; the launch traced here: 517 us
  blocking collectives  222 us (43%)
  waiting for transfers between devices  102 us (20%)
  starting transfers between devices  91 us (18%)
  matrix products  42.6 us (8%)
  local copies, waits for them, and re-layouts  34.3 us (7%)
  between operations  16.5 us (3%)
  other arithmetic  8.16 us (2%)
    psum x1, blocking collectives, on_device(): summed = lax.psum(lax.psum(weight_term, 'row'), 'col')  222 us
    psum x1, waiting for transfers between devices, on_device(): summed = lax.psum(lax.psum(weight_term, 'row'), 'col')  83.4 us
    ppermute x8, starting transfers between devices, passed_along(): lax.ppermute(value, axis, [(source, source + steps) for source in range(l...  40.7 us
    dot_general x6, matrix products, product(): return jnp.einsum(form, left, right, preferred_element_type=jnp.float32)  37.1 us
    ppermute x6, starting transfers between devices, extended(): lax.ppermute(tail, axis, [(i, (i + 1) % count) for i in range(ends)])  36.8 us
    ppermute x6, starting transfers between devices, extended(): lax.ppermute(head, axis, [((i + 1) % count, i) for i in range(ends)])  13.4 us
    ppermute x8, waiting for transfers between devices, passed_along(): lax.ppermute(value, axis, [(source, source + steps) for source in range(l...  11.9 us
  transfers between devices with their start and end apart: 23, of which 4 were waited for; matrix products, arithmetic and copies ran while one was open for 12% of the time, Pallas kernels for 0%

profile of v1, /device:TPU:47, one launch (start us, length us, event | category | flops | bytes accessed | tf_op | source)
XLA Modules:
  0.0 516.9 jit_solution(2992925853900233234)
XLA Ops:
  9.1 2.7 collective-permute-start.1
  11.8 3.1 collective-permute-start
  18.7 2.5 collective-permute-start.5
  21.2 3.1 collective-permute-start.4
  26.8 2.4 collective-permute-start.7
  29.3 8.8 %collective-permute-start.6 = (bf16[14,3]{1,0:T(8,128)(2,1)S(1)}, bf16[14,3]{1,0:T(8,128)(2,1)S(1)}, u32[]{:S(2)}, u32[]{:S(2)}) collective-permute-start(bf16[14,3]{1,0:T(8,128)(2,1)S(1)} %get-tuple-element.122), channel_id=1, source_target_pairs={{0,1},{1,2},{2,3},{3,4},{4,5},{5,6},{6,7},{7,8},{8,9},{9,10},{10,1... | collective-permute-start | bytes 260 | tf_op jit(solution)/shard_map/ppermute | solution.py:30
  38.2 3.0 collective-permute-start.8
  43.7 9.4 %collective-permute-start.2 = (bf16[14,3,768]{2,1,0:T(4,128)(2,1)S(1)}, bf16[14,3,768]{2,1,0:T(4,128)(2,1)S(1)}, u32[]{:S(2)}, u32[]{:S(2)}) collective-permute-start(bf16[14,3,768]{2,1,0:T(4,128)(2,1)S(1)} %get-tuple-element.110), channel_id=1, source_target_pairs={{0,1},{1,2},{2,3},{3,4},{4,5},{5,6},{6,7},{7,8},{8,9},{9,10},{10,1... | collective-permute-start | bytes 193544 | tf_op jit(solution)/shard_map/ppermute | solution.py:30
  55.2 9.4 %collective-permute-start.10 = (bf16[14,3,768]{2,1,0:T(4,128)(2,1)S(1)}, bf16[14,3,768]{2,1,0:T(4,128)(2,1)S(1)}, u32[]{:S(2)}, u32[]{:S(2)}) collective-permute-start(bf16[14,3,768]{2,1,0:T(4,128)(2,1)S(1)} %get-tuple-element.108), channel_id=1, source_target_pairs={{0,1},{1,2},{2,3},{3,4},{4,5},{5,6},{6,7},{7,8},{8,9},{9,10},{10,1... | collective-permute-start | bytes 193544 | tf_op jit(solution)/shard_map/ppermute | solution.py:30
  65.0 6.2 %collective-permute-done.11 = bf16[14,3,768]{2,1,0:T(4,128)(2,1)S(1)} collective-permute-done((bf16[14,3,768]{2,1,0:T(4,128)(2,1)S(1)}, bf16[14,3,768]{2,1,0:T(4,128)(2,1)S(1)}, u32[]{:S(2)}, u32[]{:S(2)}) %collective-permute-start.11) | collective-permute-done | bytes 64544 | tf_op jit(solution)/shard_map/ppermute | solution.py:32
  82.8 4.7 fusion.24
  90.7 83.4 %all-reduce.17.cloned.1.call-done = f32[768,768]{1,0:T(8,128)} async-done(((f32[768,768]{1,0:T(8,128)}), f32[768,768]{1,0:T(8,128)}) %all-reduce.17.cloned.1.call-update) | async-done | bytes 2359312 | tf_op jit(solution)/shard_map/psum | solution.py:244
  174.1 222.2 %all-reduce.18 = bf16[768,768]{1,0:T(8,128)(2,1)} all-reduce(f32[768,768]{1,0:T(8,128)} %all-reduce.17.cloned.1.call-done), channel_id=1, replica_groups=mesh['dp'=4,'row'=8,'col'=16] {'col'}, use_global_device_ids=true, to_apply=%region_4.5 | all-reduce | flops 589824 | bytes 3538944 | tf_op jit(solution)/shard_map/psum | solution.py:244
  400.6 11.4 %fusion.25 = bf16[2,64,12,64]{1,3,2,0:T(8,128)(2,1)} fusion(bf16[2,196,12,64]{1,3,2,0:T(8,128)(2,1)S(1)} %copy.80, f32[2,12,64,196]{3,2,1,0:T(8,128)} %fusion.68, f32[2,12,64,196]{3,2,1,0:T(8,128)} %get-tuple-element.127, f32[2,12,64]{2,1,0:T(8,128)S(1)} %broadcast_divide_fusion), kind=kOutput, calls=%fused_computation.21 | convolution fusion | flops 40742596 | bytes 3213312 | tf_op jit(solution)/shard_map/nhqk,nkhd->nqhd/dot_general | solution.py:40
  412.0 11.8 %fusion.12 = f32[2,196,12,64]{1,3,2,0:T(8,128)} fusion(bf16[2,64,12,64]{1,3,2,0:T(8,128)(2,1)S(1)} %copy-done.8, f32[2,12,64,196]{3,2,1,0:T(8,128)} %fusion.68, f32[2,12,64,196]{3,2,1,0:T(8,128)} %get-tuple-element.127, f32[2,12,64]{2,1,0:T(8,128)S(1)} %broadcast_divide_fusion), kind=kOutput, calls=%fused_computation.9 | convolution fusion | flops 40644292 | bytes 3815424 | tf_op jit(solution)/shard_map/nhqk,nqhd->nkhd/dot_general | solution.py:40
  423.9 3.5 copy.84
  434.2 5.9 %convolution_bitcast_fusion = f32[2,196,12,64]{1,3,2,0:T(8,128)} fusion(bf16[2,64,12,64]{1,3,2,0:T(8,128)(2,1)S(1)} %copy-done.2, f32[2,12,64]{2,1,0:T(8,128)S(1)} %broadcast_divide_fusion, f32[2,12,64,196]{3,2,1,0:T(8,128)} %bitcast_select_fusion), kind=kOutput, calls=%fused_computation.11 | convolution fusion | flops 39440068 | bytes 2611200 | tf_op jit(solution)/shard_map/nhqk,nqhd->nkhd/dot_general | solution.py:40
  440.0 3.5 copy.87
  451.3 10.1 %collective-permute-start.12 = (bf16[3,22,768]{2,1,0:T(8,128)(2,1)S(1)}, bf16[3,22,768]{2,1,0:T(8,128)(2,1)S(1)}, u32[]{:S(2)}, u32[]{:S(2)}) collective-permute-start(bf16[3,22,768]{2,1,0:T(8,128)(2,1)S(1)} %get-tuple-element.103), channel_id=1, source_target_pairs={{0,16},{16,32},{32,48},{48,64},{64,80},{80,96},{96,112},{1,17},{17... | collective-permute-start | bytes 304136 | tf_op jit(solution)/shard_map/ppermute | solution.py:15
  463.6 3.6 collective-permute-start.16
  469.4 3.9 collective-permute-done.17
  473.5 9.9 %collective-permute-start.14 = (bf16[8,3,768]{2,1,0:T(4,128)(2,1)S(1)}, bf16[8,3,768]{2,1,0:T(4,128)(2,1)S(1)}, u32[]{:S(2)}, u32[]{:S(2)}) collective-permute-start(bf16[8,3,768]{2,1,0:T(4,128)(2,1)S(1)} %get-tuple-element.115), channel_id=1, source_target_pairs={{0,1},{1,2},{2,3},{3,4},{4,5},{5,6},{6,7},{7,8},{8,9},{9,10},{10,1... | collective-permute-start | bytes 110600 | tf_op jit(solution)/shard_map/ppermute | solution.py:15
  485.4 9.4 %collective-permute-start.18 = (bf16[8,3,768]{2,1,0:T(4,128)(2,1)S(1)}, bf16[8,3,768]{2,1,0:T(4,128)(2,1)S(1)}, u32[]{:S(2)}, u32[]{:S(2)}) collective-permute-start(bf16[8,3,768]{2,1,0:T(4,128)(2,1)S(1)} %get-tuple-element.113), channel_id=1, source_target_pairs={{0,1},{1,2},{2,3},{3,4},{4,5},{5,6},{6,7},{7,8},{8,9},{9,10},{10,1... | collective-permute-start | bytes 110600 | tf_op jit(solution)/shard_map/ppermute | solution.py:15
  497.9 8.0 %collective-permute-done.19 = bf16[8,3,768]{2,1,0:T(4,128)(2,1)S(1)} collective-permute-done((bf16[8,3,768]{2,1,0:T(4,128)(2,1)S(1)}, bf16[8,3,768]{2,1,0:T(4,128)(2,1)S(1)}, u32[]{:S(2)}, u32[]{:S(2)}) %collective-permute-start.19) | collective-permute-done | bytes 36896 | tf_op jit(solution)/shard_map/ppermute | solution.py:15
  (181 shorter events, 58.5 us)
Async XLA Ops:
  8.0 166.1 %all-reduce.17.cloned.1.call-start = ((), (), s32[]{:S(2)}) async-start(), calls=%async_computation.2 | async-start | bytes 4718592 | tf_op jit(solution)/shard_map/psum | solution.py:244
  9.1 32.6 %collective-permute-start.1 = (bf16[3,16,768]{2,1,0:T(8,128)(2,1)S(1)}, bf16[3,16,768]{2,1,0:T(8,128)(2,1)S(1)}, u32[]{:S(2)}, u32[]{:S(2)}) collective-permute-start(bf16[3,16,768]{2,1,0:T(8,128)(2,1)S(1)} %get-tuple-element.119), channel_id=1, source_target_pairs={{16,0},{32,16},{48,32},{64,48},{80,64},{96,80},{112,96},{17,1},{33... | collective-permute-start | bytes 221192 | tf_op jit(solution)/shard_map/ppermute | solution.py:32
  11.8 29.9 %collective-permute-start = (bf16[3,16,768]{2,1,0:T(8,128)(2,1)S(1)}, bf16[3,16,768]{2,1,0:T(8,128)(2,1)S(1)}, u32[]{:S(2)}, u32[]{:S(2)}) collective-permute-start(bf16[3,16,768]{2,1,0:T(8,128)(2,1)S(1)} %get-tuple-element.118), channel_id=1, source_target_pairs={{0,16},{16,32},{32,48},{48,64},{64,80},{80,96},{96,112},{1,17},{17... | collective-permute-start | bytes 221192 | tf_op jit(solution)/shard_map/ppermute | solution.py:30
  15.9 37.2 %collective-permute-start.9 = (bf16[3,16,768]{2,1,0:T(8,128)(2,1)S(1)}, bf16[3,16,768]{2,1,0:T(8,128)(2,1)S(1)}, u32[]{:S(2)}, u32[]{:S(2)}) collective-permute-start(bf16[3,16,768]{2,1,0:T(8,128)(2,1)S(1)} %get-tuple-element.117), channel_id=1, source_target_pairs={{16,0},{32,16},{48,32},{64,48},{80,64},{96,80},{112,96},{17,1},{33... | collective-permute-start | bytes 221192 | tf_op jit(solution)/shard_map/ppermute | solution.py:32
  18.7 8.0 %collective-permute-start.5 = (bf16[3,16]{1,0:T(4,128)(2,1)S(1)}, bf16[3,16]{1,0:T(4,128)(2,1)S(1)}, u32[]{:S(2)}, u32[]{:S(2)}) collective-permute-start(bf16[3,16]{1,0:T(4,128)(2,1)S(1)} %get-tuple-element.125), channel_id=1, source_target_pairs={{16,0},{32,16},{48,32},{64,48},{80,64},{96,80},{112,96},{17,1},{33... | collective-permute-start | bytes 296 | tf_op jit(solution)/shard_map/ppermute | solution.py:32
  21.2 5.5 %collective-permute-start.4 = (bf16[3,16]{1,0:T(4,128)(2,1)S(1)}, bf16[3,16]{1,0:T(4,128)(2,1)S(1)}, u32[]{:S(2)}, u32[]{:S(2)}) collective-permute-start(bf16[3,16]{1,0:T(4,128)(2,1)S(1)} %get-tuple-element.124), channel_id=1, source_target_pairs={{0,16},{16,32},{32,48},{48,64},{64,80},{80,96},{96,112},{1,17},{17... | collective-permute-start | bytes 296 | tf_op jit(solution)/shard_map/ppermute | solution.py:30
  26.8 11.3 %collective-permute-start.7 = (bf16[14,3]{1,0:T(8,128)(2,1)S(1)}, bf16[14,3]{1,0:T(8,128)(2,1)S(1)}, u32[]{:S(2)}, u32[]{:S(2)}) collective-permute-start(bf16[14,3]{1,0:T(8,128)(2,1)S(1)} %get-tuple-element.123), channel_id=1, source_target_pairs={{1,0},{2,1},{3,2},{4,3},{5,4},{6,5},{7,6},{8,7},{9,8},{10,9},{11,1... | collective-permute-start | bytes 260 | tf_op jit(solution)/shard_map/ppermute | solution.py:32
  29.3 11.9 %collective-permute-start.6 = (bf16[14,3]{1,0:T(8,128)(2,1)S(1)}, bf16[14,3]{1,0:T(8,128)(2,1)S(1)}, u32[]{:S(2)}, u32[]{:S(2)}) collective-permute-start(bf16[14,3]{1,0:T(8,128)(2,1)S(1)} %get-tuple-element.122), channel_id=1, source_target_pairs={{0,1},{1,2},{2,3},{3,4},{4,5},{5,6},{6,7},{7,8},{8,9},{9,10},{10,1... | collective-permute-start | bytes 260 | tf_op jit(solution)/shard_map/ppermute | solution.py:30
  38.2 15.0 %collective-permute-start.8 = (bf16[3,16,768]{2,1,0:T(8,128)(2,1)S(1)}, bf16[3,16,768]{2,1,0:T(8,128)(2,1)S(1)}, u32[]{:S(2)}, u32[]{:S(2)}) collective-permute-start(bf16[3,16,768]{2,1,0:T(8,128)(2,1)S(1)} %get-tuple-element.116), channel_id=1, source_target_pairs={{0,16},{16,32},{32,48},{48,64},{64,80},{80,96},{96,112},{1,17},{17... | collective-permute-start | bytes 221192 | tf_op jit(solution)/shard_map/ppermute | solution.py:30
  41.8 22.7 %collective-permute-start.3 = (bf16[14,3,768]{2,1,0:T(4,128)(2,1)S(1)}, bf16[14,3,768]{2,1,0:T(4,128)(2,1)S(1)}, u32[]{:S(2)}, u32[]{:S(2)}) collective-permute-start(bf16[14,3,768]{2,1,0:T(4,128)(2,1)S(1)} %get-tuple-element.111), channel_id=1, source_target_pairs={{1,0},{2,1},{3,2},{4,3},{5,4},{6,5},{7,6},{8,7},{9,8},{10,9},{11,1... | collective-permute-start | bytes 193544 | tf_op jit(solution)/shard_map/ppermute | solution.py:32
  43.7 20.8 %collective-permute-start.2 = (bf16[14,3,768]{2,1,0:T(4,128)(2,1)S(1)}, bf16[14,3,768]{2,1,0:T(4,128)(2,1)S(1)}, u32[]{:S(2)}, u32[]{:S(2)}) collective-permute-start(bf16[14,3,768]{2,1,0:T(4,128)(2,1)S(1)} %get-tuple-element.110), channel_id=1, source_target_pairs={{0,1},{1,2},{2,3},{3,4},{4,5},{5,6},{6,7},{7,8},{8,9},{9,10},{10,1... | collective-permute-start | bytes 193544 | tf_op jit(solution)/shard_map/ppermute | solution.py:30
  53.2 18.0 %collective-permute-start.11 = (bf16[14,3,768]{2,1,0:T(4,128)(2,1)S(1)}, bf16[14,3,768]{2,1,0:T(4,128)(2,1)S(1)}, u32[]{:S(2)}, u32[]{:S(2)}) collective-permute-start(bf16[14,3,768]{2,1,0:T(4,128)(2,1)S(1)} %get-tuple-element.109), channel_id=1, source_target_pairs={{1,0},{2,1},{3,2},{4,3},{5,4},{6,5},{7,6},{8,7},{9,8},{10,9},{11,1... | collective-permute-start | bytes 193544 | tf_op jit(solution)/shard_map/ppermute | solution.py:32
  55.2 16.0 %collective-permute-start.10 = (bf16[14,3,768]{2,1,0:T(4,128)(2,1)S(1)}, bf16[14,3,768]{2,1,0:T(4,128)(2,1)S(1)}, u32[]{:S(2)}, u32[]{:S(2)}) collective-permute-start(bf16[14,3,768]{2,1,0:T(4,128)(2,1)S(1)} %get-tuple-element.108), channel_id=1, source_target_pairs={{0,1},{1,2},{2,3},{3,4},{4,5},{5,6},{6,7},{7,8},{8,9},{9,10},{10,1... | collective-permute-start | bytes 193544 | tf_op jit(solution)/shard_map/ppermute | solution.py:30
  90.0 306.3 %all-gather.2.cloned.1.call-start = ((), (), s32[]{:S(2)}) async-start(), calls=%async_computation.1 | async-start | bytes 1474560 | tf_op jit(solution)/shard_map/all_gather | solution.py:229
  90.6 417.0 %reduce-scatter.2.cloned.1.call-start = ((), (), s32[]{:S(2)}) async-start(), calls=%async_computation.3 | async-start | bytes 1474560 | tf_op jit(solution)/shard_map/reduce_scatter | solution.py:245
  90.7 305.6 %copy-start.13 = (bf16[1,8,16,768]{3,2,1,0:T(8,128)(2,1)S(1)}, bf16[1,8,16,768]{3,2,1,0:T(8,128)(2,1)}, u32[]{:S(2)}) copy-start(bf16[1,8,16,768]{3,2,1,0:T(8,128)(2,1)} %param.27) | copy-start | bytes 589828
  451.3 17.9 %collective-permute-start.12 = (bf16[3,22,768]{2,1,0:T(8,128)(2,1)S(1)}, bf16[3,22,768]{2,1,0:T(8,128)(2,1)S(1)}, u32[]{:S(2)}, u32[]{:S(2)}) collective-permute-start(bf16[3,22,768]{2,1,0:T(8,128)(2,1)S(1)} %get-tuple-element.103), channel_id=1, source_target_pairs={{0,16},{16,32},{32,48},{48,64},{64,80},{80,96},{96,112},{1,17},{17... | collective-permute-start | bytes 304136 | tf_op jit(solution)/shard_map/ppermute | solution.py:15
  461.6 7.6 %collective-permute-start.13 = (bf16[3,22,768]{2,1,0:T(8,128)(2,1)S(1)}, bf16[3,22,768]{2,1,0:T(8,128)(2,1)S(1)}, u32[]{:S(2)}, u32[]{:S(2)}) collective-permute-start(bf16[3,22,768]{2,1,0:T(8,128)(2,1)S(1)} %get-tuple-element.102), channel_id=1, source_target_pairs={{16,0},{32,16},{48,32},{64,48},{80,64},{96,80},{112,96},{17,1},{33... | collective-permute-start | bytes 304136 | tf_op jit(solution)/shard_map/ppermute | solution.py:15
  463.6 5.7 %collective-permute-start.16 = (bf16[3,22,768]{2,1,0:T(8,128)(2,1)S(1)}, bf16[3,22,768]{2,1,0:T(8,128)(2,1)S(1)}, u32[]{:S(2)}, u32[]{:S(2)}) collective-permute-start(bf16[3,22,768]{2,1,0:T(8,128)(2,1)S(1)} %get-tuple-element.101), channel_id=1, source_target_pairs={{0,16},{16,32},{32,48},{48,64},{64,80},{80,96},{96,112},{1,17},{17... | collective-permute-start | bytes 304136 | tf_op jit(solution)/shard_map/ppermute | solution.py:15
  467.3 6.1 %collective-permute-start.17 = (bf16[3,22,768]{2,1,0:T(8,128)(2,1)S(1)}, bf16[3,22,768]{2,1,0:T(8,128)(2,1)S(1)}, u32[]{:S(2)}, u32[]{:S(2)}) collective-permute-start(bf16[3,22,768]{2,1,0:T(8,128)(2,1)S(1)} %get-tuple-element.100), channel_id=1, source_target_pairs={{16,0},{32,16},{48,32},{64,48},{80,64},{96,80},{112,96},{17,1},{33... | collective-permute-start | bytes 304136 | tf_op jit(solution)/shard_map/ppermute | solution.py:15
  473.5 23.2 %collective-permute-start.14 = (bf16[8,3,768]{2,1,0:T(4,128)(2,1)S(1)}, bf16[8,3,768]{2,1,0:T(4,128)(2,1)S(1)}, u32[]{:S(2)}, u32[]{:S(2)}) collective-permute-start(bf16[8,3,768]{2,1,0:T(4,128)(2,1)S(1)} %get-tuple-element.115), channel_id=1, source_target_pairs={{0,1},{1,2},{2,3},{3,4},{4,5},{5,6},{6,7},{7,8},{8,9},{9,10},{10,1... | collective-permute-start | bytes 110600 | tf_op jit(solution)/shard_map/ppermute | solution.py:15
  483.4 13.8 %collective-permute-start.15 = (bf16[8,3,768]{2,1,0:T(4,128)(2,1)S(1)}, bf16[8,3,768]{2,1,0:T(4,128)(2,1)S(1)}, u32[]{:S(2)}, u32[]{:S(2)}) collective-permute-start(bf16[8,3,768]{2,1,0:T(4,128)(2,1)S(1)} %get-tuple-element.114), channel_id=1, source_target_pairs={{1,0},{2,1},{3,2},{4,3},{5,4},{6,5},{7,6},{8,7},{9,8},{10,9},{11,1... | collective-permute-start | bytes 110600 | tf_op jit(solution)/shard_map/ppermute | solution.py:15
  485.4 11.4 %collective-permute-start.18 = (bf16[8,3,768]{2,1,0:T(4,128)(2,1)S(1)}, bf16[8,3,768]{2,1,0:T(4,128)(2,1)S(1)}, u32[]{:S(2)}, u32[]{:S(2)}) collective-permute-start(bf16[8,3,768]{2,1,0:T(4,128)(2,1)S(1)} %get-tuple-element.113), channel_id=1, source_target_pairs={{0,1},{1,2},{2,3},{3,4},{4,5},{5,6},{6,7},{7,8},{8,9},{9,10},{10,1... | collective-permute-start | bytes 110600 | tf_op jit(solution)/shard_map/ppermute | solution.py:15
  494.8 11.1 %collective-permute-start.19 = (bf16[8,3,768]{2,1,0:T(4,128)(2,1)S(1)}, bf16[8,3,768]{2,1,0:T(4,128)(2,1)S(1)}, u32[]{:S(2)}, u32[]{:S(2)}) collective-permute-start(bf16[8,3,768]{2,1,0:T(4,128)(2,1)S(1)} %get-tuple-element.112), channel_id=1, source_target_pairs={{1,0},{2,1},{3,2},{4,3},{5,4},{6,5},{7,6},{8,7},{9,8},{10,9},{11,1... | collective-permute-start | bytes 110600 | tf_op jit(solution)/shard_map/ppermute | solution.py:15
  (18 other events, 198.7 us)
Sparse Core Ops, SparseCore 0:
  90.1 83.9 all-reduce.16
Sparse Core Ops, SparseCore 1:
  92.6 43.1 all-gather.1
  396.4 45.5 reduce-scatter.1
